TPU v7x, 32 devices: a whole 2x2x4 slice. The times are simulated.
32 devices in a mesh: range: 4 (over y, core), chan: 8 (over z, x).
Axes of the slice: x: 2, y: 2, z: 4, core: 2. Of those that a mesh axis runs over, the one named last changes fastest.
Arguments:
- echoes: float32 [2, 64, 512, 1024], P(None, 'chan', None, 'range'), may hold values from -18 to 18
- chirp: float32 [2, 129], replicated, may hold values from -0.375 to 0.375
- train_mask: int32 [512, 8], P('chan', 'range'), may hold values from 0 to 1, as said below
Outputs:
- spectra: bfloat16 [2, 512, 64, 1024], P(None, 'chan', None, 'range')
- factors: float32 [512, 2, 128, 128], P('chan')
Inputs may be any that keep to these rules, and one draw needn't show every extreme that they name: `train_mask`: in each Doppler bin exactly 4 consecutive tiles are 0 and all other tiles are 1.
All inputs are finite; a program needn't handle non-finite values.
Results may differ from a plain program's by a relative error of at most 0.001.
Values sent between devices are 32-bit elements; how exact they have to be, the bound alone decides.
A program may use at most 128 MiB of HBM per device.

v0:
```python
import math
import jax
import jax.numpy as jnp
from jax import lax
from jax.sharding import PartitionSpec as P

TILE = 128
best_precision = lax.Precision.HIGHEST


def from_behind(value, axis, steps):
    count = lax.axis_size(axis)
    leading, last = (max(0, -steps), min(count, count - steps))
    return lax.ppermute(value, axis, [(source, source + steps) for source in range(leading, last)])


def from_behind_2(block, axis, distance):
    devices = range(lax.axis_size(axis))
    route = [((i - distance) % len(devices), i) for i in devices]
    return lax.ppermute(block, axis, route)


def toeplitz_rows(taps):
    tap_span = taps.shape[-1] - 1
    padded = jnp.concatenate([taps, jnp.zeros((taps.shape[0], tap_span), taps.dtype)], -1)
    tiled = jnp.tile(padded, (1, tap_span))
    return tiled[:, : 2 * tap_span * tap_span].reshape(taps.shape[0], tap_span, 2 * tap_span)


def compress(extended, taps):
    tap_span = taps.shape[-1] - 1
    lead_shape = extended.shape[:-1]
    block_count = extended.shape[-1] // tap_span - 1
    blocks = extended.reshape(lead_shape + (block_count + 1, tap_span))
    window = jnp.concatenate([blocks[..., :block_count, :], blocks[..., 1:, :]], -1)
    kernel = toeplitz_rows(taps)
    products = jnp.einsum(
        "tcpnk,sok->tscpno",
        window,
        kernel,
        precision=best_precision,
        preferred_element_type=jnp.float32,
    )
    real_part = products[0, 0] + products[1, 1]
    imag_part = products[1, 0] - products[0, 1]
    return jnp.stack([real_part, imag_part]).reshape(lead_shape + (block_count * tap_span,))


def doppler_table(bin_numbers, pulse_count):
    phase_index = (
        bin_numbers[:, None] * jnp.arange(pulse_count, dtype=jnp.int32)[None, :] % pulse_count
    )
    angles = phase_index.astype(jnp.float32) * (2.0 * math.pi / pulse_count)
    scaling = 1.0 / math.sqrt(pulse_count)
    return jnp.stack([jnp.cos(angles) * scaling, -jnp.sin(angles) * scaling])


def doppler(signal, dft_table):
    products = jnp.einsum(
        "sdp,tcpg->stdcg",
        dft_table,
        signal,
        precision=best_precision,
        preferred_element_type=jnp.float32,
    )
    return jnp.stack([products[0, 0] - products[1, 1], products[0, 1] + products[1, 0]])


def gram_block(spectra_now, spectra_next, weights, scaling):
    snapshot = jnp.concatenate([spectra_now, spectra_next], 2)
    masked = snapshot * weights[None, :, None, :]
    products = jnp.einsum(
        "tbkg,sblg->btskl",
        masked,
        snapshot,
        precision=best_precision,
        preferred_element_type=jnp.float32,
    )
    real_part = products[:, 0, 0] + products[:, 1, 1]
    imag_part = products[:, 0, 1] - products[:, 1, 0]
    return jnp.stack([real_part, imag_part], 1) * scaling


def factor(gram):
    order_size = gram.shape[-1]
    strip_size = min(16, order_size)
    columns = jnp.arange(order_size, dtype=jnp.int32)
    remaining = gram
    pieces = []
    for offset in range(0, order_size, strip_size):
        strip_rows = remaining[:, :, :strip_size, :]

        def column_step(position, carry):
            strip_now, found_rows = carry
            place = offset + position
            row_now = lax.dynamic_index_in_dim(strip_now, position, 2, keepdims=False)
            pivots = jnp.sum(jnp.where(columns == place, row_now[:, 0], 0.0), -1)
            inverse = lax.rsqrt(pivots)[:, None]
            row_real = jnp.where(columns >= place, row_now[:, 0] * inverse, 0.0)
            row_imag = jnp.where(columns > place, row_now[:, 1] * inverse, 0.0)
            coef_real = row_real[:, offset : offset + strip_size]
            coef_imag = row_imag[:, offset : offset + strip_size]
            new_real = (
                strip_now[:, 0]
                - coef_real[:, :, None] * row_real[:, None, :]
                - coef_imag[:, :, None] * row_imag[:, None, :]
            )
            new_imag = (
                strip_now[:, 1]
                - coef_real[:, :, None] * row_imag[:, None, :]
                + coef_imag[:, :, None] * row_real[:, None, :]
            )
            found_rows = lax.dynamic_update_index_in_dim(
                found_rows, jnp.stack([row_real, row_imag], 1), position, 2
            )
            return (jnp.stack([new_real, new_imag], 1), found_rows)

        strip_end, found_rows = lax.fori_loop(
            0, strip_size, column_step, (strip_rows, jnp.zeros_like(strip_rows))
        )
        pieces.append(found_rows)
        if offset + strip_size < order_size:
            tail_part = found_rows[:, :, :, offset + strip_size :]
            products = jnp.einsum(
                "nabi,ncbj->nacij",
                tail_part,
                found_rows,
                precision=best_precision,
                preferred_element_type=jnp.float32,
            )
            update_real = products[:, 0, 0] + products[:, 1, 1]
            update_imag = products[:, 0, 1] - products[:, 1, 0]
            remaining = remaining[:, :, strip_size:, :] - jnp.stack([update_real, update_imag], 1)
    return jnp.concatenate(pieces, 2)


def on_device(echoes, chirp, train_mask):
    tap_span = chirp.shape[-1] - 1
    pulses = echoes.shape[2]
    gate_count = echoes.shape[3]
    rim_gates = from_behind(echoes[..., :tap_span], "range", -1)
    compressed = compress(jnp.concatenate([echoes, rim_gates], -1), chirp)
    spectra_all = doppler(compressed, doppler_table(jnp.arange(pulses, dtype=jnp.int32), pulses))
    turned = lax.all_to_all(spectra_all, "chan", split_axis=1, concat_axis=2, tiled=True)
    edge_bin = from_behind_2(turned[:, :1], "chan", -1)
    following = jnp.concatenate([turned[:, 1:], edge_bin], 1)
    spectra_out = turned.astype(jnp.bfloat16)
    total_gates = gate_count * lax.axis_size("range")
    scaling = 1.0 / total_gates
    weights = jnp.broadcast_to(
        train_mask.astype(jnp.float32)[:, :, None], train_mask.shape + (TILE,)
    ).reshape(train_mask.shape[0], gate_count)
    partial_gram = lax.psum_scatter(
        gram_block(turned, following, weights, scaling), "range", scatter_dimension=0, tiled=True
    )
    factors = lax.all_gather(factor(partial_gram), "range", axis=0, tiled=True)
    return (spectra_out, factors)


def solution(mesh):
    return jax.shard_map(
        on_device,
        mesh=mesh,
        in_specs=(P(None, "chan", None, "range"), P(), P("chan", "range")),
        out_specs=(P(None, "chan", None, "range"), P("chan", None, None, None)),
        check_vma=False,
    )
```

profile of v0, /device:TPU:0, one launch (start us, length us, event | category | flops | bytes accessed | tf_op | source)
XLA Modules:
  0.0 662.5 jit_solution(18391180482651036311)
XLA Ops:
  7.2 8.7 %copy.189 = f32[2,8,512,256]{2,3,1,0:T(8,128)} copy(f32[2,8,512,256]{3,2,1,0:T(8,128)} %param.19) | data formatting | bytes 16777216 | tf_op args[0]
  15.9 4.8 slice.757
  20.7 1.3 collective-permute-start
  22.6 4.2 negate_multiply_fusion
  26.7 3.4 collective-permute-done
  30.1 6.2 pad_maximum_fusion.8
  36.3 7.0 %fusion.104 = (f32[2,8,512,2,128]{2,4,3,1,0:T(8,128)}, f32[2,8,512,2,128]{2,4,3,1,0:T(8,128)}) fusion(f32[2,8,512,3,128]{2,4,3,1,0:T(8,128)S(1)} %bitcast.399), kind=kLoop, calls=%fused_computation.288 | loop fusion | bytes 33554432 | tf_op jit(solution)/shard_map/slice | solution.py:35
  43.3 8.7 %copy.286 = f32[2,8,512,2,128]{4,2,3,1,0:T(8,128)} copy(f32[2,8,512,2,128]{2,4,3,1,0:T(8,128)} %get-tuple-element.1093) | data formatting | bytes 16777216
  52.0 8.7 %copy.285 = f32[2,8,512,2,128]{4,2,3,1,0:T(8,128)} copy(f32[2,8,512,2,128]{2,4,3,1,0:T(8,128)} %get-tuple-element.1092) | data formatting | bytes 16777216
  60.7 21.7 %fusion.55 = f32[2,2,8,512,2,128]{3,5,4,2,0,1:T(8,128)} fusion(f32[2,8,512,2,128]{4,2,3,1,0:T(8,128)} %copy.286, f32[2,8,512,2,128]{4,2,3,1,0:T(8,128)} %copy.285, f32[1,2,128,256]{3,1,2,0:T(2,128)S(1)} %bitcast.450), kind=kOutput, calls=%fused_computation.179 | convolution fusion | flops 12889096192 | bytes 33816576 | tf_op jit(solution)/shard_map/tcpnk,sok->tscpno/dot_general | solution.py:37
  82.5 10.2 %slice_add_fusion.1 = (f32[1,1,8,512,2,128]{3,5,4,2,0,1:T(8,128)S(1)}, f32[1,1,8,512,2,128]{3,5,4,2,0,1:T(8,128)}) fusion(f32[2,2,8,512,2,128]{3,5,4,2,0,1:T(8,128)} %fusion.55), kind=kLoop, calls=%fused_computation.194 | loop fusion | flops 2097152 | bytes 25165824 | tf_op jit(solution)/shard_map/add | solution.py:44
  92.6 31.7 %fusion.56 = f32[2,2,512,8,256]{2,4,0,3,1:T(8,128)S(1)} fusion(f32[1,8,512,256]{2,3,1,0:T(8,128)} %bitcast.409, f32[1,8,512,256]{2,3,1,0:T(8,128)S(1)} %bitcast.408, f32[1,512,512]{2,1,0:T(8,128)S(1)} %get-tuple-element.1118, f32[1,512,512]{2,1,0:T(8,128)S(1)} %get-tuple-element.1119), kind=kOutput, calls=%fused_computation.180 | convolution fusion | flops 25772425216 | bytes 27262976 | tf_op jit(solution)/shard_map/sdp,tcpg->stdcg/dot_general | solution.py:59
  126.4 4.4 pad_maximum_fusion.9
  130.7 10.3 %copy.194 = f32[2,512,8,256]{3,2,0,1:T(8,128)} copy(f32[2,512,8,256]{1,3,2,0:T(8,128)} %pad_maximum_fusion.9) | data formatting | bytes 16777216 | tf_op jit(solution)/shard_map/stack | solution.py:66
  141.1 177.9 %all_to_all.18 = f32[2,512,8,256]{3,2,0,1:T(8,128)S(1)} all-to-all(f32[2,512,8,256]{3,2,0,1:T(8,128)} %copy.194), channel_id=1, replica_groups=mesh['range'=4,'chan'=8] {'chan'}, dimensions={1} | all-to-all | bytes 16777216 | tf_op jit(solution)/shard_map/all_to_all | solution.py:144
  319.0 1.3 copy.366
  320.3 2.2 copy-done
  322.5 3.3 copy-done.1
  325.8 3.1 collective-permute-start.1
  329.2 7.6 %slice.768 = f32[2,63,64,256]{3,2,0,1:T(8,128)} slice(f32[2,64,64,256]{3,2,0,1:T(8,128)} %bitcast.402), slice={[0:2], [1:64], [0:64], [0:256]} | slice | bytes 16515072 | tf_op jit(solution)/shard_map/slice | solution.py:146
  336.8 27.5 %fusion.46 = f32[64,2,2,128,128]{3,4,1,2,0:T(8,128)} fusion(f32[2,1,64,256]{3,2,0,1:T(8,128)S(1)} %collective-permute-done.1, f32[2,63,64,256]{3,2,0,1:T(8,128)} %slice.768, f32[2,64,64,256]{3,2,0,1:T(8,128)} %bitcast.403, f32[64,256]{1,0:T(8,128)S(1)} %bitcast.452), kind=kOutput, calls=%fused_computation.169 | convolution fusion | flops 12905873408 | bytes 33619968 | tf_op jit(solution)/shard_map/tbkg,sblg->btskl/dot_general | solution.py:72
  364.3 4.2 fusion.57
  368.5 4.2 fusion.59
  372.8 1.6 maximum_multiply_fusion
  375.5 8.0 %copy.365 = f32[8,8,256,128]{3,1,2,0:T(8,128)} copy(f32[8,8,256,128]{3,2,1,0:T(8,128)S(1)} %bitcast.404) | data formatting | bytes 16777216
  383.6 82.1 %reduce-scatter.5.cloned.1.call-done = f32[16,32768]{1,0:T(8,128)} async-done(((f32[64,32768]{1,0:T(8,128)}), f32[16,32768]{1,0:T(8,128)}) %reduce-scatter.5.cloned.1.call-update) | async-done | bytes 2097168
  465.7 2.0 copy.300
  467.7 1.9 slice.775
  470.2 8.8 %while.136 = (s32[]{:T(128)}, f32[16,2,16,128]{3,2,1,0:T(8,128)S(1)}, f32[16,2,16,128]{3,0,1,2:T(8,128)S(1)}, s32[]{:T(128)}) while((s32[]{:T(128)}, f32[16,2,16,128]{3,2,1,0:T(8,128)S(1)}, f32[16,2,16,128]{3,0,1,2:T(8,128)S(1)}, s32[]{:T(128)}) %tuple.404), condition=%wide.region_3.4_spmd.clone.clone, body=%wide.region_1.3_spmd.clone.clone.sunk | while | flops 345458 | bytes 1227949 | solution.py:118
  479.9 3.3 convolution_bitcast_fusion
  484.3 1.7 copy.292
  486.1 1.9 maximum_subtract_fusion
  488.1 11.2 %while.137 = (s32[]{:T(128)}, f32[16,2,16,128]{3,2,1,0:T(8,128)S(1)}, f32[16,2,16,128]{3,0,1,2:T(8,128)S(1)}, s32[]{:T(128)}, s32[]{:T(128)}) while((s32[]{:T(128)}, f32[16,2,16,128]{3,2,1,0:T(8,128)S(1)}, f32[16,2,16,128]{3,0,1,2:T(8,128)S(1)}, s32[]{:T(128)}, s32[]{:T(128)}) %tuple.407), condition=%wide.region_6.7_spmd.clone.clone, body=%wide.region_4.6_spmd.clone.clone.sunk | while | flops 345459 | bytes 1228033 | solution.py:118
  500.1 2.9 convolution_bitcast_fusion.1
  504.7 11.2 %while.138 = (s32[]{:T(128)}, f32[16,2,16,128]{3,2,1,0:T(8,128)S(1)}, f32[16,2,16,128]{3,0,1,2:T(8,128)S(1)}, s32[]{:T(128)}, s32[]{:T(128)}) while((s32[]{:T(128)}, f32[16,2,16,128]{3,2,1,0:T(8,128)S(1)}, f32[16,2,16,128]{3,0,1,2:T(8,128)S(1)}, s32[]{:T(128)}, s32[]{:T(128)}) %tuple.410), condition=%wide.region_9.10_spmd.clone.clone, body=%wide.region_7.9_spmd.clone.clone.sunk | while | flops 345459 | bytes 1228033 | solution.py:118
  516.8 2.4 convolution_bitcast_fusion.2
  519.6 11.4 %while.139 = (s32[]{:T(128)}, f32[16,2,16,128]{3,2,1,0:T(8,128)S(1)}, f32[16,2,16,128]{3,0,1,2:T(8,128)S(1)}, s32[]{:T(128)}, s32[]{:T(128)}) while((s32[]{:T(128)}, f32[16,2,16,128]{3,2,1,0:T(8,128)S(1)}, f32[16,2,16,128]{3,0,1,2:T(8,128)S(1)}, s32[]{:T(128)}, s32[]{:T(128)}) %tuple.413), condition=%wide.region_12.13_spmd.clone.clone, body=%wide.region_10.12_spmd.clone.clone.sunk | while | flops 345459 | bytes 1228033 | solution.py:118
  531.9 2.0 convolution_bitcast_fusion.3
  534.4 11.2 %while.140 = (s32[]{:T(128)}, f32[16,2,16,128]{3,2,1,0:T(8,128)S(1)}, f32[16,2,16,128]{3,0,1,2:T(8,128)S(1)}, s32[]{:T(128)}, s32[]{:T(128)}) while((s32[]{:T(128)}, f32[16,2,16,128]{3,2,1,0:T(8,128)S(1)}, f32[16,2,16,128]{3,0,1,2:T(8,128)S(1)}, s32[]{:T(128)}, s32[]{:T(128)}) %tuple.416), condition=%wide.region_15.16_spmd.clone.clone, body=%wide.region_13.15_spmd.clone.clone.sunk | while | flops 345459 | bytes 1228033 | solution.py:118
  546.4 1.6 convolution_bitcast_fusion.4
  548.3 11.2 %while.141 = (s32[]{:T(128)}, f32[16,2,16,128]{3,2,1,0:T(8,128)S(1)}, f32[16,2,16,128]{3,0,1,2:T(8,128)S(1)}, s32[]{:T(128)}, s32[]{:T(128)}) while((s32[]{:T(128)}, f32[16,2,16,128]{3,2,1,0:T(8,128)S(1)}, f32[16,2,16,128]{3,0,1,2:T(8,128)S(1)}, s32[]{:T(128)}, s32[]{:T(128)}) %tuple.419), condition=%wide.region_18.19_spmd.clone.clone, body=%wide.region_16.18_spmd.clone.clone.sunk | while | flops 345459 | bytes 1228033 | solution.py:118
  560.4 1.3 convolution_bitcast_fusion.5
  561.9 11.2 %while.142 = (s32[]{:T(128)}, f32[16,2,16,128]{3,2,1,0:T(8,128)S(1)}, f32[16,2,16,128]{3,0,1,2:T(8,128)S(1)}, s32[]{:T(128)}, s32[]{:T(128)}) while((s32[]{:T(128)}, f32[16,2,16,128]{3,2,1,0:T(8,128)S(1)}, f32[16,2,16,128]{3,0,1,2:T(8,128)S(1)}, s32[]{:T(128)}, s32[]{:T(128)}) %tuple.422), condition=%wide.region_21.22_spmd.clone.clone, body=%wide.region_19.21_spmd.clone.clone.sunk | while | flops 345459 | bytes 1228033 | solution.py:118
  575.4 13.0 %while.143 = (s32[]{:T(128)}, f32[16,2,16,128]{3,2,1,0:T(8,128)S(1)}, f32[16,2,16,128]{3,2,1,0:T(8,128)S(1)}, s32[]{:T(128)}, s32[]{:T(128)}, /*index=5*/s32[]{:T(128)}) while((s32[]{:T(128)}, f32[16,2,16,128]{3,2,1,0:T(8,128)S(1)}, f32[16,2,16,128]{3,2,1,0:T(8,128)S(1)}, s32[]{:T(128)}, s32[]{:T(128)}, ...), condition=%wide.region_24.25_spmd.clone.clone, body=%wide.region_22.24_spmd.clone.clone.sunk | while | flops 345459 | bytes 1293577 | solution.py:118
  589.2 4.0 copy.368
  593.2 2.3 copy.239
  595.5 52.1 %all-gather.2.cloned.1.call-done = f32[64,2,128,128]{3,2,1,0:T(8,128)} async-done(((f32[16,2,128,128]{3,2,1,0:T(8,128)}), f32[64,2,128,128]{3,2,1,0:T(8,128)}) %all-gather.2.cloned.1.call-update) | async-done | bytes 8388624 | tf_op jit(solution)/shard_map/all_gather | solution.py:156
  647.6 7.9 %copy.476 = f32[64,2,128,128]{3,2,1,0:T(8,128)} copy(f32[64,2,128,128]{3,2,1,0:T(8,128)} %all-gather.2.cloned.1.call-done) | data formatting | bytes 16777216
  (1742 shorter events, 96.3 us)
Async XLA Ops:
  7.2 458.5 %reduce-scatter.5.cloned.1.call-start = ((), (), s32[]{:S(2)}) async-start(), calls=%async_computation.3 | async-start | bytes 10485760
  15.9 6.1 copy-start.6
  20.7 9.4 %collective-permute-start = (f32[2,8,512,128]{2,3,1,0:T(8,128)}, f32[2,8,512,128]{2,3,1,0:T(8,128)}, u32[]{:S(2)}, u32[]{:S(2)}) collective-permute-start(f32[2,8,512,128]{2,3,1,0:T(8,128)} %slice.757), channel_id=1, source_target_pairs={{8,0},{16,8},{24,16},{9,1},{17,9},{25,17},{10,2},{18,10},{26,18},{... | collective-permute-start | bytes 12582920 | tf_op jit(solution)/shard_map/ppermute | solution.py:14
  22.6 13.7 %copy-start.5 = (f32[2,32896]{1,0:T(2,128)}, f32[2,32896]{1,0:T(2,128)S(1)}, u32[]{:S(2)}) copy-start(f32[2,32896]{1,0:T(2,128)S(1)} %tile.10) | copy-start | bytes 789508
  52.0 8.7 %slice-start = ((f32[2,32896]{1,0:T(2,128)}), f32[2,32768]{1,0:T(2,128)S(1)}, s32[]{:S(2)}) async-start(f32[2,32896]{1,0:T(2,128)} %copy-done.5), calls=%async_computation.4 | async-start | bytes 524288 | tf_op jit(solution)/shard_map/slice | solution.py:27
  319.0 3.5 copy-start
  319.0 9.9 %copy-start.7 = (s32[64,2]{0,1:T(2,128)S(1)}, s32[64,2]{0,1:T(2,128)}, u32[]{:S(2)}) copy-start(s32[64,2]{0,1:T(2,128)} %param.21) | copy-start | bytes 1540
  322.5 3.3 copy-start.1
  325.8 11.0 %collective-permute-start.1 = (f32[2,1,64,256]{3,2,0,1:T(8,128)S(1)}, f32[2,1,64,256]{3,2,0,1:T(8,128)S(1)}, u32[]{:S(2)}, u32[]{:S(2)}) collective-permute-start(f32[2,1,64,256]{3,2,0,1:T(8,128)S(1)} %slice.769), channel_id=1, source_target_pairs={{1,0},{2,1},{3,2},{4,3},{5,4},{6,5},{7,6},{0,7},{9,8},{10,9},{11,1... | collective-permute-start | bytes 393224 | tf_op jit(solution)/shard_map/ppermute | solution.py:20
  383.6 264.0 %all-gather.2.cloned.1.call-start = ((), (), s32[]{:S(2)}) async-start(), calls=%async_computation.2 | async-start | bytes 10485760 | tf_op jit(solution)/shard_map/all_gather | solution.py:156
  479.9 4.4 copy-start.2
  503.5 1.1 copy-start.3
  515.9 3.5 copy-start.4
Sparse Core Ops, SparseCore 0:
  383.7 81.9 reduce-scatter.4
  589.3 58.2 all-gather.1
where the time goes:
time: 668 us; the launch traced here: 663 us
  blocking collectives  178 us (27%)
  waiting for transfers between devices  138 us (21%)
  local copies, waits for them, and re-layouts  124 us (19%)
  other arithmetic  98.7 us (15%)
  matrix products  95.1 us (14%)
  between operations  14.8 us (2%)
  loops' own time  9.7 us (1%)
    all_to_all x1, blocking collectives, on_device(): lax.all_to_all(spectra_all, 'chan', split_axis=1, concat_axis=2, tiled=True)  178 us
    unnamed x3, waiting for transfers between devices  82.1 us
    unnamed x35, local copies, waits for them, and re-layouts  57.4 us
    all_gather x1, waiting for transfers between devices, on_device(): factors = lax.all_gather(factor(partial_gram), 'range', axis=0, tiled=True)  52.1 us
    dot_general x1, matrix products, doppler(): jnp.einsum('sdp,tcpg->stdcg', dft_table, signal, precision=best_precision...  31.7 us
    dot_general x1, matrix products, gram_block(): jnp.einsum('tbkg,sblg->btskl', masked, snapshot, precision=best_precision...  27.5 us
    dot_general x1, matrix products, compress(): jnp.einsum('tcpnk,sok->tscpno', window, kernel, precision=best_precision,...  21.7 us
    select_n x256, other arithmetic, column_step(): row_real = jnp.where(columns >= place, row_now[:, 0] * inverse, 0.0)  19 us
  transfers between devices with their start and end apart: 4, of which 3 were waited for; matrix products, arithmetic and copies ran while one was open for 3% of the time, Pallas kernels for 0%

commit v1 on v0

--- a/solution.py
+++ b/solution.py
@@ -141,7 +141,12 @@
     rim_gates = from_behind(echoes[..., :tap_span], "range", -1)
     compressed = compress(jnp.concatenate([echoes, rim_gates], -1), chirp)
     spectra_all = doppler(compressed, doppler_table(jnp.arange(pulses, dtype=jnp.int32), pulses))
-    turned = lax.all_to_all(spectra_all, "chan", split_axis=1, concat_axis=2, tiled=True)
+    turned = jnp.concatenate(
+        lax.all_to_all(
+            jnp.stack(jnp.split(spectra_all, lax.axis_size("chan"), axis=1)), "chan", 0, 0
+        ),
+        axis=2,
+    )
     edge_bin = from_behind_2(turned[:, :1], "chan", -1)
     following = jnp.concatenate([turned[:, 1:], edge_bin], 1)
     spectra_out = turned.astype(jnp.bfloat16)

time: 668 us -> 680 us (1.018)
  other arithmetic: 98.7 us -> 108 us
    unnamed x0 -> x7, other arithmetic: none -> 12.4 us
    unnamed x35 -> x34, local copies, waits for them, and re-layouts: 57.4 us -> 59.9 us
where the time goes in v1:
time: 680 us; the launch traced here: 675 us
  blocking collectives  178 us (26%)
  waiting for transfers between devices  138 us (20%)
  local copies, waits for them, and re-layouts  128 us (19%)
  other arithmetic  108 us (16%)
  matrix products  93.8 us (14%)
  between operations  15.1 us (2%)
  loops' own time  9.84 us (1%)
    all_to_all x1, blocking collectives, on_device(): lax.all_to_all(jnp.stack(jnp.split(spectra_all, lax.axis_size('chan'), ax...  178 us
    unnamed x3, waiting for transfers between devices  82.1 us
    unnamed x34, local copies, waits for them, and re-layouts  59.9 us
    all_gather x1, waiting for transfers between devices, on_device(): factors = lax.all_gather(factor(partial_gram), 'range', axis=0, tiled=True)  52.4 us
    dot_general x1, matrix products, doppler(): jnp.einsum('sdp,tcpg->stdcg', dft_table, signal, precision=best_precision...  31.9 us
    dot_general x1, matrix products, gram_block(): jnp.einsum('tbkg,sblg->btskl', masked, snapshot, precision=best_precision...  26 us
    dot_general x1, matrix products, compress(): jnp.einsum('tcpnk,sok->tscpno', window, kernel, precision=best_precision,...  21.7 us
    select_n x256, other arithmetic, column_step(): row_real = jnp.where(columns >= place, row_now[:, 0] * inverse, 0.0)  19 us
  transfers between devices with their start and end apart: 4, of which 3 were waited for; matrix products, arithmetic and copies ran while one was open for 3% of the time, Pallas kernels for 0%

profile of v1, /device:TPU:0, one launch (start us, length us, event | category | flops | bytes accessed | tf_op | source)
XLA Modules:
  0.0 674.7 jit_solution(15937365246078017848)
XLA Ops:
  7.2 8.7 %copy.190 = f32[2,8,512,256]{2,3,1,0:T(8,128)} copy(f32[2,8,512,256]{3,2,1,0:T(8,128)} %param.19) | data formatting | bytes 16777216 | tf_op args[0]
  15.9 4.8 slice.757
  22.6 4.2 negate_multiply_fusion
  26.7 3.4 collective-permute-done
  30.1 6.2 pad_maximum_fusion.8
  36.3 7.0 %fusion.127 = (f32[2,8,512,2,128]{2,4,3,1,0:T(8,128)}, f32[2,8,512,2,128]{2,4,3,1,0:T(8,128)}) fusion(f32[2,8,512,3,128]{2,4,3,1,0:T(8,128)S(1)} %bitcast.433), kind=kLoop, calls=%fused_computation.325 | loop fusion | bytes 33554432 | tf_op jit(solution)/shard_map/slice | solution.py:35
  43.3 8.7 %copy.286 = f32[2,8,512,2,128]{4,2,3,1,0:T(8,128)} copy(f32[2,8,512,2,128]{2,4,3,1,0:T(8,128)} %get-tuple-element.1086) | data formatting | bytes 16777216
  52.0 8.7 %copy.287 = f32[2,8,512,2,128]{4,2,3,1,0:T(8,128)} copy(f32[2,8,512,2,128]{2,4,3,1,0:T(8,128)} %get-tuple-element.1087) | data formatting | bytes 16777216
  60.7 21.7 %fusion.55 = f32[2,2,8,512,2,128]{3,5,4,2,0,1:T(8,128)} fusion(f32[2,8,512,2,128]{4,2,3,1,0:T(8,128)} %copy.287, f32[2,8,512,2,128]{4,2,3,1,0:T(8,128)} %copy.286, f32[1,2,128,256]{3,1,2,0:T(2,128)S(1)} %bitcast.483), kind=kOutput, calls=%fused_computation.192 | convolution fusion | flops 12889096192 | bytes 33816576 | tf_op jit(solution)/shard_map/tcpnk,sok->tscpno/dot_general | solution.py:37
  82.4 10.2 %slice_add_fusion.1 = (f32[1,1,8,512,2,128]{3,5,4,2,0,1:T(8,128)S(1)}, f32[1,1,8,512,2,128]{3,5,4,2,0,1:T(8,128)}) fusion(f32[2,2,8,512,2,128]{3,5,4,2,0,1:T(8,128)} %fusion.55), kind=kLoop, calls=%fused_computation.207 | loop fusion | flops 2097152 | bytes 25165824 | tf_op jit(solution)/shard_map/add | solution.py:44
  92.6 31.9 %fusion.56 = f32[2,2,512,8,256]{2,4,0,3,1:T(8,128)S(1)} fusion(f32[1,8,512,256]{2,3,1,0:T(8,128)} %bitcast.441, f32[1,8,512,256]{2,3,1,0:T(8,128)S(1)} %bitcast.440, f32[1,512,512]{2,1,0:T(8,128)S(1)} %get-tuple-element.1112, f32[1,512,512]{2,1,0:T(8,128)S(1)} %get-tuple-element.1113), kind=kOutput, calls=%fused_computation.193 | convolution fusion | flops 25772425216 | bytes 27262976 | tf_op jit(solution)/shard_map/sdp,tcpg->stdcg/dot_general | solution.py:59
  128.2 1.9 fusion.71
  130.1 1.7 fusion.74
  131.8 2.0 fusion.77
  135.4 2.0 fusion.83
  139.0 1.9 fusion.85
  140.9 12.8 %copy.195 = f32[8,2,64,8,256]{4,3,2,1,0:T(8,128)} copy(f32[8,2,64,8,256]{2,4,3,1,0:T(8,128)} %fusion.85) | data formatting | bytes 16777216 | tf_op jit(solution)/shard_map/stack | solution.py:146
  153.7 177.9 %all_to_all.5 = f32[8,2,64,8,256]{4,3,2,1,0:T(8,128)S(1)} all-to-all(f32[8,2,64,8,256]{4,3,2,1,0:T(8,128)} %copy.195), channel_id=1, replica_groups=mesh['range'=4,'chan'=8] {'chan'}, dimensions={0} | all-to-all | bytes 16777216 | tf_op jit(solution)/shard_map/all_to_all | solution.py:145
  332.9 2.2 copy-done
  335.1 3.3 copy-done.1
  338.4 3.1 collective-permute-start.1
  341.8 3.9 slice.768
  345.7 3.8 copy.381
  349.5 26.0 %fusion.46 = f32[64,2,2,128,128]{3,4,1,2,0:T(8,128)} fusion(f32[2,1,64,256]{3,2,0,1:T(8,128)S(1)} %collective-permute-done.1, f32[2,63,64,256]{3,2,0,1:T(8,128)} %copy.381, f32[64,256]{1,0:T(8,128)S(1)} %bitcast.485, f32[8,2,64,8,256]{4,3,2,1,0:T(8,128)} %copy-done), kind=kOutput, calls=%fused_computation.183 | convolution fusion | flops 12905873408 | bytes 33619968 | tf_op jit(solution)/shard_map/tbkg,sblg->btskl/dot_general | solution.py:72
  375.5 4.2 fusion.57
  379.8 4.2 fusion.59
  384.0 1.6 maximum_multiply_fusion
  386.8 8.0 %copy.376 = f32[8,8,256,128]{3,1,2,0:T(8,128)} copy(f32[8,8,256,128]{3,2,1,0:T(8,128)S(1)} %bitcast.437) | data formatting | bytes 16777216
  394.9 82.0 %reduce-scatter.5.cloned.1.call-done = f32[16,32768]{1,0:T(8,128)} async-done(((f32[64,32768]{1,0:T(8,128)}), f32[16,32768]{1,0:T(8,128)}) %reduce-scatter.5.cloned.1.call-update) | async-done | bytes 2097168
  476.9 2.0 copy.301
  479.5 8.8 %while.136 = (s32[]{:T(128)}, f32[16,2,16,128]{3,2,1,0:T(8,128)S(1)}, f32[16,2,16,128]{3,0,1,2:T(8,128)S(1)}, s32[]{:T(128)}) while((s32[]{:T(128)}, f32[16,2,16,128]{3,2,1,0:T(8,128)S(1)}, f32[16,2,16,128]{3,0,1,2:T(8,128)S(1)}, s32[]{:T(128)}) %tuple.401), condition=%wide.region_3.4_spmd.clone.clone, body=%wide.region_1.3_spmd.clone.clone.sunk | while | flops 345458 | bytes 1227941 | solution.py:118
  489.2 3.3 convolution_bitcast_fusion
  493.6 1.9 slice.775
  495.6 2.8 copy.293
  498.4 1.9 maximum_subtract_fusion
  500.4 11.1 %while.137 = (s32[]{:T(128)}, f32[16,2,16,128]{3,2,1,0:T(8,128)S(1)}, f32[16,2,16,128]{3,0,1,2:T(8,128)S(1)}, s32[]{:T(128)}, s32[]{:T(128)}) while((s32[]{:T(128)}, f32[16,2,16,128]{3,2,1,0:T(8,128)S(1)}, f32[16,2,16,128]{3,0,1,2:T(8,128)S(1)}, s32[]{:T(128)}, s32[]{:T(128)}) %tuple.404), condition=%wide.region_6.7_spmd.clone.clone, body=%wide.region_4.6_spmd.clone.clone.sunk | while | flops 345459 | bytes 1228025 | solution.py:118
  512.4 2.9 convolution_bitcast_fusion.1
  517.0 11.1 %while.138 = (s32[]{:T(128)}, f32[16,2,16,128]{3,2,1,0:T(8,128)S(1)}, f32[16,2,16,128]{3,0,1,2:T(8,128)S(1)}, s32[]{:T(128)}, s32[]{:T(128)}) while((s32[]{:T(128)}, f32[16,2,16,128]{3,2,1,0:T(8,128)S(1)}, f32[16,2,16,128]{3,0,1,2:T(8,128)S(1)}, s32[]{:T(128)}, s32[]{:T(128)}) %tuple.407), condition=%wide.region_9.10_spmd.clone.clone, body=%wide.region_7.9_spmd.clone.clone.sunk | while | flops 345459 | bytes 1228025 | solution.py:118
  529.0 2.4 convolution_bitcast_fusion.2
  531.8 11.4 %while.139 = (s32[]{:T(128)}, f32[16,2,16,128]{3,2,1,0:T(8,128)S(1)}, f32[16,2,16,128]{3,0,1,2:T(8,128)S(1)}, s32[]{:T(128)}, s32[]{:T(128)}) while((s32[]{:T(128)}, f32[16,2,16,128]{3,2,1,0:T(8,128)S(1)}, f32[16,2,16,128]{3,0,1,2:T(8,128)S(1)}, s32[]{:T(128)}, s32[]{:T(128)}) %tuple.410), condition=%wide.region_12.13_spmd.clone.clone, body=%wide.region_10.12_spmd.clone.clone.sunk | while | flops 345459 | bytes 1228025 | solution.py:118
  544.1 2.0 convolution_bitcast_fusion.3
  546.5 11.1 %while.140 = (s32[]{:T(128)}, f32[16,2,16,128]{3,2,1,0:T(8,128)S(1)}, f32[16,2,16,128]{3,0,1,2:T(8,128)S(1)}, s32[]{:T(128)}, s32[]{:T(128)}) while((s32[]{:T(128)}, f32[16,2,16,128]{3,2,1,0:T(8,128)S(1)}, f32[16,2,16,128]{3,0,1,2:T(8,128)S(1)}, s32[]{:T(128)}, s32[]{:T(128)}) %tuple.413), condition=%wide.region_15.16_spmd.clone.clone, body=%wide.region_13.15_spmd.clone.clone.sunk | while | flops 345459 | bytes 1228025 | solution.py:118
  560.4 11.1 %while.141 = (s32[]{:T(128)}, f32[16,2,16,128]{3,2,1,0:T(8,128)S(1)}, f32[16,2,16,128]{3,0,1,2:T(8,128)S(1)}, s32[]{:T(128)}, s32[]{:T(128)}) while((s32[]{:T(128)}, f32[16,2,16,128]{3,2,1,0:T(8,128)S(1)}, f32[16,2,16,128]{3,0,1,2:T(8,128)S(1)}, s32[]{:T(128)}, s32[]{:T(128)}) %tuple.416), condition=%wide.region_18.19_spmd.clone.clone, body=%wide.region_16.18_spmd.clone.clone.sunk | while | flops 345459 | bytes 1228025 | solution.py:118
  574.0 11.1 %while.142 = (s32[]{:T(128)}, f32[16,2,16,128]{3,2,1,0:T(8,128)S(1)}, f32[16,2,16,128]{3,0,1,2:T(8,128)S(1)}, s32[]{:T(128)}, s32[]{:T(128)}) while((s32[]{:T(128)}, f32[16,2,16,128]{3,2,1,0:T(8,128)S(1)}, f32[16,2,16,128]{3,0,1,2:T(8,128)S(1)}, s32[]{:T(128)}, s32[]{:T(128)}) %tuple.419), condition=%wide.region_21.22_spmd.clone.clone, body=%wide.region_19.21_spmd.clone.clone.sunk | while | flops 345459 | bytes 1228025 | solution.py:118
  586.6 12.9 %while.143 = (s32[]{:T(128)}, f32[16,2,16,128]{3,2,1,0:T(8,128)S(1)}, f32[16,2,16,128]{3,2,1,0:T(8,128)S(1)}, s32[]{:T(128)}, s32[]{:T(128)}, /*index=5*/s32[]{:T(128)}) while((s32[]{:T(128)}, f32[16,2,16,128]{3,2,1,0:T(8,128)S(1)}, f32[16,2,16,128]{3,2,1,0:T(8,128)S(1)}, s32[]{:T(128)}, s32[]{:T(128)}, ...), condition=%wide.region_24.25_spmd.clone.clone, body=%wide.region_22.24_spmd.clone.clone.sunk | while | flops 345459 | bytes 1293569 | solution.py:118
  601.1 6.1 copy.379
  607.2 52.4 %all-gather.2.cloned.1.call-done = f32[64,2,128,128]{3,2,1,0:T(8,128)} async-done(((f32[16,2,128,128]{3,2,1,0:T(8,128)}), f32[64,2,128,128]{3,2,1,0:T(8,128)}) %all-gather.2.cloned.1.call-update) | async-done | bytes 8388624 | tf_op jit(solution)/shard_map/all_gather | solution.py:161
  659.6 7.9 %copy.496 = f32[64,2,128,128]{3,2,1,0:T(8,128)} copy(f32[64,2,128,128]{3,2,1,0:T(8,128)} %all-gather.2.cloned.1.call-done) | data formatting | bytes 16777216
  (1748 shorter events, 106.1 us)
Async XLA Ops:
  7.2 469.7 %reduce-scatter.5.cloned.1.call-start = ((), (), s32[]{:S(2)}) async-start(), calls=%async_computation.3 | async-start | bytes 10485760
  15.9 6.1 copy-start.5
  20.7 9.4 %collective-permute-start = (f32[2,8,512,128]{2,3,1,0:T(8,128)}, f32[2,8,512,128]{2,3,1,0:T(8,128)}, u32[]{:S(2)}, u32[]{:S(2)}) collective-permute-start(f32[2,8,512,128]{2,3,1,0:T(8,128)} %slice.757), channel_id=1, source_target_pairs={{8,0},{16,8},{24,16},{9,1},{17,9},{25,17},{10,2},{18,10},{26,18},{... | collective-permute-start | bytes 12582920 | tf_op jit(solution)/shard_map/ppermute | solution.py:14
  22.6 13.7 %copy-start.4 = (f32[2,32896]{1,0:T(2,128)}, f32[2,32896]{1,0:T(2,128)S(1)}, u32[]{:S(2)}) copy-start(f32[2,32896]{1,0:T(2,128)S(1)} %tile.10) | copy-start | bytes 789508
  52.0 8.7 %slice-start = ((f32[2,32896]{1,0:T(2,128)}), f32[2,32768]{1,0:T(2,128)S(1)}, s32[]{:S(2)}) async-start(f32[2,32896]{1,0:T(2,128)} %copy-done.4), calls=%async_computation.4 | async-start | bytes 524288 | tf_op jit(solution)/shard_map/slice | solution.py:27
  331.6 3.5 copy-start
  331.6 9.9 %copy-start.6 = (s32[64,2]{0,1:T(2,128)S(1)}, s32[64,2]{0,1:T(2,128)}, u32[]{:S(2)}) copy-start(s32[64,2]{0,1:T(2,128)} %param.21) | copy-start | bytes 1540
  335.1 3.3 copy-start.1
  338.4 11.1 %collective-permute-start.1 = (f32[2,1,64,256]{3,2,0,1:T(8,128)S(1)}, f32[2,1,64,256]{3,2,0,1:T(8,128)S(1)}, u32[]{:S(2)}, u32[]{:S(2)}) collective-permute-start(f32[2,1,64,256]{3,2,0,1:T(8,128)S(1)} %copy.380), channel_id=1, source_target_pairs={{1,0},{2,1},{3,2},{4,3},{5,4},{6,5},{7,6},{0,7},{9,8},{10,9},{11,1... | collective-permute-start | bytes 393224 | tf_op jit(solution)/shard_map/ppermute | solution.py:20
  394.8 264.8 %all-gather.2.cloned.1.call-start = ((), (), s32[]{:S(2)}) async-start(), calls=%async_computation.2 | async-start | bytes 10485760 | tf_op jit(solution)/shard_map/all_gather | solution.py:161
  515.7 1.1 copy-start.2
  528.1 3.5 copy-start.3
Sparse Core Ops, SparseCore 0:
  394.9 81.9 reduce-scatter.4
  601.3 58.2 all-gather.1
